TPU v7x, 32 devices: a whole 2x2x4 slice. The times are simulated.
32 devices in a mesh: row: 8 (over z, x), col: 4 (over y, core).
Axes of the slice: x: 2, y: 2, z: 4, core: 2. Of those that a mesh axis runs over, the one named last changes fastest.
Arguments:
- tokens: bfloat16 [512, 4096], P('row', 'col'), may hold values from -6 to 6
- gate_weight: bfloat16 [4096, 14336], P('col', 'row'), may hold values from -0.09375 to 0.09375
- up_weight: bfloat16 [4096, 14336], P('col', 'row'), may hold values from -0.09375 to 0.09375
- down_weight: bfloat16 [14336, 4096], P('row', 'col'), may hold values from -0.046875 to 0.046875
- gate_mask: int32 [32, 112], replicated, may hold values 0 or 1
- up_mask: int32 [32, 112], replicated, may hold values 0 or 1
- down_mask: int32 [112, 32], replicated, may hold values 0 or 1
- out_grad: bfloat16 [512, 4096], P('row', 'col'), may hold values from -6 to 6
Outputs:
- mixed: bfloat16 [512, 4096], P('row', 'col')
- input_grad: bfloat16 [512, 4096], P('row', 'col')
- gate_grad: float32 [4096, 14336], P('col', 'row')
- up_grad: float32 [4096, 14336], P('col', 'row')
- down_grad: float32 [14336, 4096], P('row', 'col')
All inputs are finite; a program needn't handle non-finite values.
Results may differ from a plain program's by a relative error of at most 0.0049.
Values may be sent and summed in bfloat16 or wider, within the bound.
No kernel may reach another device: no remote copies, remote signals or barrier semaphores. Data moves between devices by JAX's collectives and lax.ppermute only.
A program may use at most 128 MiB of HBM per device.

v0:
```python
import jax
import jax.numpy as jnp
from jax import lax
from jax.sharding import PartitionSpec as P

BLOCK = 128


def expand_mask(mask, row_start, row_count, col_start, col_count):
    row_block = (row_start + lax.broadcasted_iota(jnp.int32, (row_count, 1), 0)) // BLOCK
    left = (row_block == lax.broadcasted_iota(jnp.int32, (1, mask.shape[0]), 1)).astype(jnp.float32)
    col_block = (col_start + lax.broadcasted_iota(jnp.int32, (1, col_count), 1)) // BLOCK
    right = (lax.broadcasted_iota(jnp.int32, (mask.shape[1], 1), 0) == col_block).astype(
        jnp.float32
    )
    middle = jnp.dot(left, mask.astype(jnp.float32), precision=lax.Precision.HIGHEST)
    return jnp.dot(middle, right, precision=lax.Precision.HIGHEST)


def contract_first(left, right):
    return lax.dot_general(
        left, right, (((0,), (0,)), ((), ())), preferred_element_type=jnp.float32
    )


def contract_last(left, right):
    return lax.dot_general(
        left, right, (((1,), (1,)), ((), ())), preferred_element_type=jnp.float32
    )


def per_device(
    tokens, gate_weight, up_weight, down_weight, gate_mask, up_mask, down_mask, out_grad
):
    row_index = lax.axis_index("row")
    col_index = lax.axis_index("col")
    feat_cols = gate_weight.shape[0]
    unit_cols = gate_weight.shape[1]
    keep_gate = expand_mask(
        gate_mask, col_index * feat_cols, feat_cols, row_index * unit_cols, unit_cols
    )
    keep_up = expand_mask(
        up_mask, col_index * feat_cols, feat_cols, row_index * unit_cols, unit_cols
    )
    keep_down = expand_mask(
        down_mask, row_index * unit_cols, unit_cols, col_index * feat_cols, feat_cols
    )
    zero = jnp.zeros((), jnp.bfloat16)
    kept_both = jnp.concatenate(
        [jnp.where(keep_gate > 0, gate_weight, zero), jnp.where(keep_up > 0, up_weight, zero)],
        axis=1,
    )
    kept_down = jnp.where(keep_down > 0, down_weight, zero)
    gathered = lax.all_gather(tokens, "row", axis=0, tiled=True)
    block = gathered
    both = lax.psum_scatter(
        jnp.dot(block, kept_both, preferred_element_type=jnp.float32),
        "col",
        scatter_dimension=0,
        tiled=True,
    )
    gate = both[:, :unit_cols]
    up_part = both[:, unit_cols:]
    sig = jax.nn.sigmoid(gate)
    hidden = (gate * sig * up_part).astype(jnp.bfloat16)
    hidden_all = lax.all_gather(hidden, "col", axis=0, tiled=True)
    block = hidden_all
    mixed = lax.psum_scatter(
        jnp.dot(block, kept_down, preferred_element_type=jnp.float32),
        "row",
        scatter_dimension=0,
        tiled=True,
    ).astype(jnp.bfloat16)
    grad_all = lax.all_gather(out_grad, "row", axis=0, tiled=True)
    down_grad = keep_down * contract_first(hidden_all, grad_all)
    block = grad_all
    hidden_grad = lax.psum_scatter(
        contract_last(block, kept_down), "col", scatter_dimension=0, tiled=True
    )
    dgate = hidden_grad * up_part * sig * (1.0 + gate * (1.0 - sig))
    dup = hidden_grad * gate * sig
    pre_grad = jnp.concatenate([dgate.astype(jnp.bfloat16), dup.astype(jnp.bfloat16)], axis=1)
    pre_all = lax.all_gather(pre_grad, "col", axis=0, tiled=True)
    weight_both = contract_first(gathered, pre_all)
    gate_grad = keep_gate * weight_both[:, :unit_cols]
    up_grad = keep_up * weight_both[:, unit_cols:]
    block = pre_all
    input_grad = lax.psum_scatter(
        contract_last(block, kept_both), "row", scatter_dimension=0, tiled=True
    ).astype(jnp.bfloat16)
    return (mixed, input_grad, gate_grad, up_grad, down_grad)


def solution(mesh):
    return jax.shard_map(
        per_device,
        mesh=mesh,
        in_specs=(
            P("row", "col"),
            P("col", "row"),
            P("col", "row"),
            P("row", "col"),
            P(),
            P(),
            P(),
            P("row", "col"),
        ),
        out_specs=(
            P("row", "col"),
            P("row", "col"),
            P("col", "row"),
            P("col", "row"),
            P("row", "col"),
        ),
        check_vma=False,
    )
```

profile of v0, /device:TPU:0, one launch (start us, length us, event | category | flops | bytes accessed | tf_op | source)
XLA Modules:
  0.0 412.9 jit_solution(11120879040870394195)
XLA Ops:
  7.2 0.0 all-gather.9.cloned.1.call-start
  7.2 0.7 all-gather.9.cloned.1.call-update
  7.9 0.0 all-gather.5.cloned.1.call-start
  7.9 0.7 all-gather.5.cloned.1.call-update
  8.7 0.0 reduce-scatter.9.cloned.1.call-start
  8.7 1.4 fusion.1
  10.1 5.0 %fusion.11 = f32[1792,1024]{1,0:T(8,128)} fusion(f32[1792,32]{1,0:T(8,128)S(1)} %fusion.1, s32[1024]{0:T(1024)S(1)} %add_select_fusion.1), kind=kOutput, calls=%fused_computation.30 | convolution fusion | flops 704675840 | bytes 7573504 | tf_op jit(solution)/shard_map/dot_general | solution.py:17
  15.2 38.0 %all-gather.9.cloned.1.call-done = bf16[512,1024]{1,0:T(8,128)(2,1)} async-done(((bf16[64,1024]{1,0:T(8,128)(2,1)}), bf16[512,1024]{1,0:T(8,128)(2,1)}) %all-gather.9.cloned.1.call-update) | async-done | bytes 1048592 | tf_op jit(solution)/shard_map/all_gather | solution.py:74
  53.1 8.3 %convolution_bitcast_fusion.2 = f32[512,1792]{0,1:T(8,128)} fusion(bf16[512,1024]{1,0:T(8,128)(2,1)} %all-gather.9.cloned.1.call-done, bf16[1792,1024]{1,0:T(8,128)(2,1)} %param.11, f32[1792,1024]{1,0:T(8,128)} %fusion.11), kind=kOutput, calls=%fused_computation.10 | convolution fusion | flops 1882718208 | bytes 15728640 | tf_op jit(solution)/shard_map/dot_general | solution.py:27
  61.4 0.0 reduce-scatter.9.cloned.1.call-update
  61.4 0.2 reduce-scatter.5.cloned.1.call-start
  61.7 0.5 copy-done.1
  62.1 0.5 fusion.4
  62.6 0.0 copy-done.2
  62.6 0.5 fusion.5
  63.1 0.0 copy-start
  63.1 7.6 %compare_select_fusion.2 = (bf16[1024,1792]{1,0:T(8,128)(2,1)}, f32[1024,1792]{1,0:T(8,128)}) fusion(bf16[1024,1792]{1,0:T(8,128)(2,1)} %param.9, f32[1024,112]{1,0:T(8,128)S(1)} %fusion.5, s32[1792]{0:T(1024)S(1)} %add_select_fusion), kind=kOutput, calls=%fused_computation.6 | convolution fusion | flops 2470121472 | bytes 15145984 | tf_op jit(solution)/shard_map/dot_general | solution.py:17
  70.7 0.0 copy-done
  70.7 5.9 %compare_select_fusion.1 = (bf16[1024,1792]{1,0:T(8,128)(2,1)}, f32[1024,1792]{1,0:T(8,128)}) fusion(bf16[1024,1792]{1,0:T(8,128)(2,1)S(1)} %copy-done, f32[1024,112]{1,0:T(8,128)S(1)} %fusion.4, s32[1792]{0:T(1024)S(1)} %add_select_fusion), kind=kOutput, calls=%fused_computation.5 | convolution fusion | flops 2470121472 | bytes 15145984 | tf_op jit(solution)/shard_map/dot_general | solution.py:17
  76.6 17.7 %all-gather.5.cloned.1.call-done = bf16[512,1024]{1,0:T(8,128)(2,1)} async-done(((bf16[64,1024]{1,0:T(8,128)(2,1)}), bf16[512,1024]{1,0:T(8,128)(2,1)}) %all-gather.5.cloned.1.call-update) | async-done | bytes 1048592 | tf_op jit(solution)/shard_map/all_gather | solution.py:54
  94.3 11.0 %convolution_bitcast_fusion.1 = f32[512,3584]{0,1:T(8,128)} fusion(bf16[512,1024]{1,0:T(8,128)(2,1)} %all-gather.5.cloned.1.call-done, bf16[1024,1792]{1,0:T(8,128)(2,1)} %get-tuple-element.10, bf16[1024,1792]{1,0:T(8,128)(2,1)} %get-tuple-element.12), kind=kOutput, calls=%fused_computation.7 | convolution fusion | flops 3772776448 | bytes 15728640 | tf_op jit(solution)/shard_map/dot_general | solution.py:57
  105.2 0.0 reduce-scatter.5.cloned.1.call-update
  105.3 0.0 all-gather.7.cloned.1.call-start
  105.3 31.3 %reduce-scatter.9.cloned.1.call-done = f32[128,1792]{0,1:T(8,128)} async-done(((f32[512,1792]{0,1:T(8,128)}), f32[128,1792]{0,1:T(8,128)}) %reduce-scatter.9.cloned.1.call-update) | async-done | bytes 917520 | tf_op jit(solution)/shard_map/reduce_scatter | solution.py:77
  136.6 67.0 %reduce-scatter.5.cloned.1.call-done = f32[128,3584]{0,1:T(8,128)} async-done(((f32[512,3584]{0,1:T(8,128)}), f32[128,3584]{0,1:T(8,128)}) %reduce-scatter.5.cloned.1.call-update) | async-done | bytes 1835024 | tf_op jit(solution)/shard_map/reduce_scatter | solution.py:56
  203.7 3.1 multiply_convert_fusion.1
  206.7 0.0 all-gather.7.cloned.1.call-update
  206.8 0.0 all-gather.11.cloned.1.call-start
  206.8 1.0 pad_maximum_fusion.3
  207.8 0.0 all-gather.11.cloned.1.call-update
  207.9 0.0 reduce-scatter.7.cloned.1.call-start
  207.9 20.3 %all-gather.7.cloned.1.call-done = bf16[512,1792]{0,1:T(8,128)(2,1)} async-done(((bf16[128,1792]{0,1:T(8,128)(2,1)}), bf16[512,1792]{0,1:T(8,128)(2,1)}) %all-gather.7.cloned.1.call-update) | async-done | bytes 1835024 | tf_op jit(solution)/shard_map/all_gather | solution.py:66
  228.2 8.2 %fusion.24 = f32[512,1024]{1,0:T(8,128)} fusion(bf16[512,1792]{0,1:T(8,128)(2,1)} %all-gather.7.cloned.1.call-done, bf16[1792,1024]{1,0:T(8,128)(2,1)} %param.11, f32[1792,1024]{1,0:T(8,128)} %fusion.11), kind=kOutput, calls=%fused_computation.55 | convolution fusion | flops 1882718208 | bytes 14942208 | tf_op jit(solution)/shard_map/dot_general | solution.py:69
  236.4 0.0 reduce-scatter.7.cloned.1.call-update
  236.4 0.3 reduce-scatter.11.cloned.1.call-start
  236.7 24.9 %all-gather.11.cloned.1.call-done = bf16[512,3584]{0,1:T(8,128)(2,1)} async-done(((bf16[128,3584]{0,1:T(8,128)(2,1)}), bf16[512,3584]{0,1:T(8,128)(2,1)}) %all-gather.11.cloned.1.call-update) | async-done | bytes 3670032 | tf_op jit(solution)/shard_map/all_gather | solution.py:83
  261.6 9.5 %fusion = f32[512,1024]{1,0:T(8,128)} fusion(bf16[512,3584]{0,1:T(8,128)(2,1)} %all-gather.11.cloned.1.call-done, bf16[1024,1792]{1,0:T(8,128)(2,1)} %get-tuple-element.10, bf16[1024,1792]{1,0:T(8,128)(2,1)} %get-tuple-element.12), kind=kOutput, calls=%fused_computation.8 | convolution fusion | flops 3772776448 | bytes 13107200 | tf_op jit(solution)/shard_map/dot_general | solution.py:27
  271.2 0.0 reduce-scatter.11.cloned.1.call-update
  271.2 0.0 copy-start.3
  271.2 0.0 slice-start.1
  271.2 9.4 %convolution_multiply_fusion = f32[1792,1024]{1,0:T(8,128)} fusion(f32[1792,1024]{1,0:T(8,128)} %fusion.11, bf16[512,1792]{0,1:T(8,128)(2,1)} %all-gather.7.cloned.1.call-done, bf16[512,1024]{1,0:T(8,128)(2,1)} %all-gather.9.cloned.1.call-done), kind=kOutput, calls=%fused_computation.9 | convolution fusion | flops 1880883200 | bytes 17563648 | tf_op jit(solution)/shard_map/dot_general | solution.py:21
  280.6 0.0 copy-done.3
  280.6 7.6 %convolution_bitcast_fusion = f32[1024,3584]{1,0:T(8,128)} fusion(bf16[512,3584]{0,1:T(8,128)(2,1)S(1)} %copy-done.3, bf16[512,1024]{1,0:T(8,128)(2,1)S(1)} %copy-done.4), kind=kOutput, calls=%fused_computation | convolution fusion | flops 3758096384 | bytes 19398656 | tf_op jit(solution)/shard_map/dot_general | solution.py:21
  288.2 14.1 %slice_multiply_fusion = (f32[1024,1792]{1,0:T(8,128)}, f32[1024,1792]{1,0:T(8,128)}) fusion(f32[1024,1792]{1,0:T(8,128)} %get-tuple-element.11, f32[1024,3584]{1,0:T(8,128)} %convolution_bitcast_fusion, f32[1024,1792]{1,0:T(8,128)S(1)} %bitcast.18), kind=kLoop, calls=%fused_computation.1 | loop fusion | flops 3670016 | bytes 44040192 | tf_op jit(solution)/shard_map/mul | solution.py:86
  302.3 31.2 %reduce-scatter.7.cloned.1.call-done = f32[64,1024]{1,0:T(8,128)} async-done(((f32[512,1024]{1,0:T(8,128)}), f32[64,1024]{1,0:T(8,128)}) %reduce-scatter.7.cloned.1.call-update) | async-done | bytes 262160 | tf_op jit(solution)/shard_map/reduce_scatter | solution.py:68
  333.5 1.6 convert_element_type.34
  335.1 69.3 %reduce-scatter.11.cloned.1.call-done = f32[64,1024]{1,0:T(8,128)} async-done(((f32[512,1024]{1,0:T(8,128)}), f32[64,1024]{1,0:T(8,128)}) %reduce-scatter.11.cloned.1.call-update) | async-done | bytes 262160 | tf_op jit(solution)/shard_map/reduce_scatter | solution.py:88
  404.5 1.6 convert_element_type.37
  (10 shorter events, 0.0 us)
Async XLA Ops:
  7.2 46.0 %all-gather.9.cloned.1.call-start = ((), (), s32[]{:S(2)}) async-start(), calls=%async_computation.8 | async-start | bytes 1179648 | tf_op jit(solution)/shard_map/all_gather | solution.py:74
  7.9 86.4 %all-gather.5.cloned.1.call-start = ((), (), s32[]{:S(2)}) async-start(), calls=%async_computation.4 | async-start | bytes 1179648 | tf_op jit(solution)/shard_map/all_gather | solution.py:54
  8.7 128.0 %reduce-scatter.9.cloned.1.call-start = ((), (), s32[]{:S(2)}) async-start(), calls=%async_computation.9 | async-start | bytes 4587520 | tf_op jit(solution)/shard_map/reduce_scatter | solution.py:77
  61.4 0.7 copy-start.1
  61.4 1.2 copy-start.2
  61.4 142.2 %reduce-scatter.5.cloned.1.call-start = ((), (), s32[]{:S(2)}) async-start(), calls=%async_computation.5 | async-start | bytes 9175040 | tf_op jit(solution)/shard_map/reduce_scatter | solution.py:56
  63.1 7.6 %copy-start = (bf16[1024,1792]{1,0:T(8,128)(2,1)S(1)}, bf16[1024,1792]{1,0:T(8,128)(2,1)}, u32[]{:S(2)}) copy-start(bf16[1024,1792]{1,0:T(8,128)(2,1)} %param.10) | copy-start | bytes 11010052
  105.3 123.0 %all-gather.7.cloned.1.call-start = ((), (), s32[]{:S(2)}) async-start(), calls=%async_computation.6 | async-start | bytes 2293760 | tf_op jit(solution)/shard_map/all_gather | solution.py:66
  206.8 54.9 %all-gather.11.cloned.1.call-start = ((), (), s32[]{:S(2)}) async-start(), calls=%async_computation.10 | async-start | bytes 4587520 | tf_op jit(solution)/shard_map/all_gather | solution.py:83
  207.9 125.6 %reduce-scatter.7.cloned.1.call-start = ((), (), s32[]{:S(2)}) async-start(), calls=%async_computation.7 | async-start | bytes 2359296 | tf_op jit(solution)/shard_map/reduce_scatter | solution.py:68
  236.4 168.0 %reduce-scatter.11.cloned.1.call-start = ((), (), s32[]{:S(2)}) async-start(), calls=%async_computation.11 | async-start | bytes 2359296 | tf_op jit(solution)/shard_map/reduce_scatter | solution.py:88
  271.2 17.0 %slice-start = ((s8[7340032]{0:T(1024)(128)(4,1)}), s8[3145728]{0:T(1024)(128)(4,1)S(1)}, s32[]{:S(2)}) async-start(s8[7340032]{0:T(1024)(128)(4,1)} %bitcast.17), calls=%async_computation.12 | async-start | bytes 6291456
  271.2 9.4 %copy-start.3 = (bf16[512,3584]{0,1:T(8,128)(2,1)S(1)}, bf16[512,3584]{0,1:T(8,128)(2,1)}, u32[]{:S(2)}) copy-start(bf16[512,3584]{0,1:T(8,128)(2,1)} %all-gather.11.cloned.1.call-done) | copy-start | bytes 11010052
  271.2 9.4 %copy-start.4 = (bf16[512,1024]{1,0:T(8,128)(2,1)S(1)}, bf16[512,1024]{1,0:T(8,128)(2,1)}, u32[]{:S(2)}) copy-start(bf16[512,1024]{1,0:T(8,128)(2,1)} %all-gather.5.cloned.1.call-done) | copy-start | bytes 3145732
  271.2 17.0 %slice-start.1 = ((s8[7340032]{0:T(1024)(128)(4,1)}), s8[4194304]{0:T(1024)(128)(4,1)S(1)}, s32[]{:S(2)}) async-start(s8[7340032]{0:T(1024)(128)(4,1)} %bitcast.17), calls=%async_computation.13 | async-start | bytes 8388608
Sparse Core Ops, SparseCore 0:
  10.1 42.9 all-gather.8
  55.3 38.9 all-gather.4
  96.8 39.7 reduce-scatter.8
  139.0 64.6 reduce-scatter.4
  206.9 21.3 all-gather.6
  229.6 31.9 all-gather.10
  265.2 68.2 reduce-scatter.6
  337.0 67.3 reduce-scatter.10
where the time goes:
time: 413 us
  waiting for transfers between devices  301 us (73%)
  matrix products  74.7 us (18%)
  other arithmetic  21.4 us (5%)
  between operations  14.2 us (3%)
    reduce_scatter x1, waiting for transfers between devices, per_device(): lax.psum_scatter(contract_last(block, kept_both), 'row', scatter_dimensio...  69.3 us
    reduce_scatter x1, waiting for transfers between devices, per_device(): lax.psum_scatter(jnp.dot(block, kept_both, preferred_element_type=jnp.flo...  67 us
    all_gather x1, waiting for transfers between devices, per_device(): grad_all = lax.all_gather(out_grad, 'row', axis=0, tiled=True)  38 us
    reduce_scatter x1, waiting for transfers between devices, per_device(): lax.psum_scatter(contract_last(block, kept_down), 'col', scatter_dimensio...  31.3 us
    reduce_scatter x1, waiting for transfers between devices, per_device(): lax.psum_scatter(jnp.dot(block, kept_down, preferred_element_type=jnp.flo...  31.2 us
    all_gather x1, waiting for transfers between devices, per_device(): pre_all = lax.all_gather(pre_grad, 'col', axis=0, tiled=True)  24.9 us
    all_gather x1, waiting for transfers between devices, per_device(): hidden_all = lax.all_gather(hidden, 'col', axis=0, tiled=True)  20.3 us
    dot_general x3, matrix products, expand_mask(): return jnp.dot(middle, right, precision=lax.Precision.HIGHEST)  18.6 us
  transfers between devices with their start and end apart: 8, of which 8 were waited for; matrix products, arithmetic and copies ran while one was open for 22% of the time, Pallas kernels for 0%

commit v1 on v0

--- a/solution.py
+++ b/solution.py
@@ -4,6 +4,19 @@
 from jax.sharding import PartitionSpec as P
 
 BLOCK = 128
+
+
+def pass_local_data(sheet):
+    parts_n = lax.axis_size("col")
+    t_next = sorted(((dev_j, (dev_j + 1) % parts_n) for dev_j in range(parts_n)))
+    then = sheet
+    trail = [then]
+    for i0 in range(1, parts_n):
+        then = lax.ppermute(then, "col", t_next)
+        trail.insert(0, then)
+    met_up = jnp.concatenate(trail, axis=0)
+    piece_out = lax.axis_index("col") + 1
+    return jnp.roll(met_up, piece_out * sheet.shape[0], axis=0)
 
 
 def expand_mask(mask, row_start, row_count, col_start, col_count):
@@ -80,7 +93,7 @@
     dgate = hidden_grad * up_part * sig * (1.0 + gate * (1.0 - sig))
     dup = hidden_grad * gate * sig
     pre_grad = jnp.concatenate([dgate.astype(jnp.bfloat16), dup.astype(jnp.bfloat16)], axis=1)
-    pre_all = lax.all_gather(pre_grad, "col", axis=0, tiled=True)
+    pre_all = pass_local_data(pre_grad)
     weight_both = contract_first(gathered, pre_all)
     gate_grad = keep_gate * weight_both[:, :unit_cols]
     up_grad = keep_up * weight_both[:, unit_cols:]

time: 413 us -> 397 us (0.961)
  waiting for transfers between devices: 301 us -> 282 us
  local copies, waits for them, and re-layouts: 0.49 us -> 7.17 us
    ppermute x0 -> x3, waiting for transfers between devices: none -> 36.9 us  [pass_local_data(): then = lax.ppermute(then, 'col', t_next)]
    all_gather x1 -> x0, waiting for transfers between devices: 24.9 us -> none  [per_device(): pre_all = lax.all_gather(pre_grad, 'col', axis=0, tiled=True)]
    all_gather x1, waiting for transfers between devices: 20.3 us -> 0.01 us  [per_device(): hidden_all = lax.all_gather(hidden, 'col', axis=0, tiled=True)]
    reduce_scatter x1, waiting for transfers between devices: 31.2 us -> 20.1 us  [per_device(): lax.psum_scatter(jnp.dot(block, kept_down, preferred_element_type=jnp.flo...]
    unnamed x14 -> x26, local copies, waits for them, and re-layouts: 0.49 us -> 7.17 us
  transfers between devices with their start and end apart: 8 -> 10, of which waited for: 8 -> 9; matrix products, arithmetic and copies ran while one was open for 22% -> 23% of each run, Pallas kernels for 0% -> 0%
where the time goes in v1:
time: 397 us
  waiting for transfers between devices  282 us (71%)
  matrix products  71.2 us (18%)
  other arithmetic  21 us (5%)
  between operations  14.3 us (4%)
  local copies, waits for them, and re-layouts  7.17 us (2%)
    reduce_scatter x1, waiting for transfers between devices, per_device(): lax.psum_scatter(contract_last(block, kept_both), 'row', scatter_dimensio...  69.3 us
    reduce_scatter x1, waiting for transfers between devices, per_device(): lax.psum_scatter(jnp.dot(block, kept_both, preferred_element_type=jnp.flo...  67 us
    all_gather x1, waiting for transfers between devices, per_device(): grad_all = lax.all_gather(out_grad, 'row', axis=0, tiled=True)  38 us
    ppermute x3, waiting for transfers between devices, pass_local_data(): then = lax.ppermute(then, 'col', t_next)  36.9 us
    reduce_scatter x1, waiting for transfers between devices, per_device(): lax.psum_scatter(contract_last(block, kept_down), 'col', scatter_dimensio...  31.3 us
    reduce_scatter x1, waiting for transfers between devices, per_device(): lax.psum_scatter(jnp.dot(block, kept_down, preferred_element_type=jnp.flo...  20.1 us
    dot_general x3, matrix products, expand_mask(): return jnp.dot(middle, right, precision=lax.Precision.HIGHEST)  18.6 us
    all_gather x1, waiting for transfers between devices, per_device(): gathered = lax.all_gather(tokens, 'row', axis=0, tiled=True)  18.1 us
  transfers between devices with their start and end apart: 10, of which 9 were waited for; matrix products, arithmetic and copies ran while one was open for 23% of the time, Pallas kernels for 0%

profile of v1, /device:TPU:0, one launch (start us, length us, event | category | flops | bytes accessed | tf_op | source)
XLA Modules:
  0.0 396.7 jit_solution(16815893431431324009)
XLA Ops:
  7.2 0.0 all-gather.8.cloned.1.call-start
  7.2 0.7 all-gather.8.cloned.1.call-update
  7.9 0.0 all-gather.4.cloned.1.call-start
  7.9 0.7 all-gather.4.cloned.1.call-update
  8.7 0.0 reduce-scatter.9.cloned.1.call-start
  8.7 1.4 fusion.3
  10.1 5.0 %fusion.13 = f32[1792,1024]{1,0:T(8,128)} fusion(f32[1792,32]{1,0:T(8,128)S(1)} %fusion.3, s32[1024]{0:T(1024)S(1)} %add_select_fusion.1), kind=kOutput, calls=%fused_computation.32 | convolution fusion | flops 704675840 | bytes 7573504 | tf_op jit(solution)/shard_map/dot_general | solution.py:30
  15.2 38.0 %all-gather.8.cloned.1.call-done = bf16[512,1024]{1,0:T(8,128)(2,1)} async-done(((bf16[64,1024]{1,0:T(8,128)(2,1)}), bf16[512,1024]{1,0:T(8,128)(2,1)}) %all-gather.8.cloned.1.call-update) | async-done | bytes 1048592 | tf_op jit(solution)/shard_map/all_gather | solution.py:87
  53.1 8.3 %convolution_bitcast_fusion.2 = f32[512,1792]{0,1:T(8,128)} fusion(bf16[512,1024]{1,0:T(8,128)(2,1)} %all-gather.8.cloned.1.call-done, bf16[1792,1024]{1,0:T(8,128)(2,1)} %param.11, f32[1792,1024]{1,0:T(8,128)} %fusion.13), kind=kOutput, calls=%fused_computation.10 | convolution fusion | flops 1882718208 | bytes 15728640 | tf_op jit(solution)/shard_map/dot_general | solution.py:40
  61.4 0.0 reduce-scatter.9.cloned.1.call-update
  61.4 0.2 reduce-scatter.5.cloned.1.call-start
  61.7 0.5 fusion.6
  62.2 0.5 fusion.7
  62.6 7.6 %compare_select_fusion.2 = (bf16[1024,1792]{1,0:T(8,128)(2,1)}, f32[1024,1792]{1,0:T(8,128)}) fusion(bf16[1024,1792]{1,0:T(8,128)(2,1)} %param.9, f32[1024,112]{1,0:T(8,128)S(1)} %fusion.7, s32[1792]{0:T(1024)S(1)} %add_select_fusion), kind=kOutput, calls=%fused_computation.6 | convolution fusion | flops 2470121472 | bytes 15145984 | tf_op jit(solution)/shard_map/dot_general | solution.py:30
  70.2 5.9 %compare_select_fusion.1 = (bf16[1024,1792]{1,0:T(8,128)(2,1)}, f32[1024,1792]{1,0:T(8,128)}) fusion(bf16[1024,1792]{1,0:T(8,128)(2,1)S(1)} %copy-done, f32[1024,112]{1,0:T(8,128)S(1)} %fusion.6, s32[1792]{0:T(1024)S(1)} %add_select_fusion), kind=kOutput, calls=%fused_computation.5 | convolution fusion | flops 2470121472 | bytes 15145984 | tf_op jit(solution)/shard_map/dot_general | solution.py:30
  76.2 18.1 %all-gather.4.cloned.1.call-done = bf16[512,1024]{1,0:T(8,128)(2,1)} async-done(((bf16[64,1024]{1,0:T(8,128)(2,1)}), bf16[512,1024]{1,0:T(8,128)(2,1)}) %all-gather.4.cloned.1.call-update) | async-done | bytes 1048592 | tf_op jit(solution)/shard_map/all_gather | solution.py:67
  94.3 11.0 %convolution_bitcast_fusion.1 = f32[512,3584]{0,1:T(8,128)} fusion(bf16[512,1024]{1,0:T(8,128)(2,1)} %all-gather.4.cloned.1.call-done, bf16[1024,1792]{1,0:T(8,128)(2,1)} %get-tuple-element.10, bf16[1024,1792]{1,0:T(8,128)(2,1)} %get-tuple-element.12), kind=kOutput, calls=%fused_computation.7 | convolution fusion | flops 3772776448 | bytes 15728640 | tf_op jit(solution)/shard_map/dot_general | solution.py:70
  105.2 0.0 reduce-scatter.5.cloned.1.call-update
  105.3 0.0 all-gather.6.cloned.1.call-start
  105.3 31.3 %reduce-scatter.9.cloned.1.call-done = f32[128,1792]{0,1:T(8,128)} async-done(((f32[512,1792]{0,1:T(8,128)}), f32[128,1792]{0,1:T(8,128)}) %reduce-scatter.9.cloned.1.call-update) | async-done | bytes 917520 | tf_op jit(solution)/shard_map/reduce_scatter | solution.py:90
  136.6 67.0 %reduce-scatter.5.cloned.1.call-done = f32[128,3584]{0,1:T(8,128)} async-done(((f32[512,3584]{0,1:T(8,128)}), f32[128,3584]{0,1:T(8,128)}) %reduce-scatter.5.cloned.1.call-update) | async-done | bytes 1835024 | tf_op jit(solution)/shard_map/reduce_scatter | solution.py:69
  203.7 3.1 multiply_convert_fusion.1
  206.7 0.0 all-gather.6.cloned.1.call-update
  206.8 0.0 reduce-scatter.7.cloned.1.call-start
  206.8 0.1 pad_maximum_fusion.3
  206.9 0.1 collective-permute-start
  207.0 18.8 %collective-permute-done = bf16[128,3584]{0,1:T(8,128)(2,1)S(1)} collective-permute-done((bf16[128,3584]{0,1:T(8,128)(2,1)S(1)}, bf16[128,3584]{0,1:T(8,128)(2,1)S(1)}, u32[]{:S(2)}, u32[]{:S(2)}) %collective-permute-start) | collective-permute-done | bytes 917536 | tf_op jit(solution)/shard_map/ppermute | solution.py:15
  225.8 13.6 %collective-permute-done.1 = bf16[128,3584]{0,1:T(8,128)(2,1)S(1)} collective-permute-done((bf16[128,3584]{0,1:T(8,128)(2,1)S(1)}, bf16[128,3584]{0,1:T(8,128)(2,1)S(1)}, u32[]{:S(2)}, u32[]{:S(2)}) %collective-permute-start.1) | collective-permute-done | bytes 917536 | tf_op jit(solution)/shard_map/ppermute | solution.py:15
  239.4 8.2 %fusion.28 = f32[512,1024]{1,0:T(8,128)} fusion(bf16[512,1792]{0,1:T(8,128)(2,1)} %all-gather.6.cloned.1.call-done, bf16[1792,1024]{1,0:T(8,128)(2,1)} %param.11, f32[1792,1024]{1,0:T(8,128)} %fusion.13), kind=kOutput, calls=%fused_computation.67 | convolution fusion | flops 1882718208 | bytes 14942208 | tf_op jit(solution)/shard_map/dot_general | solution.py:82
  247.6 0.3 reduce-scatter.11.cloned.1.call-start
  247.9 4.4 %collective-permute-done.2 = bf16[128,3584]{0,1:T(8,128)(2,1)} collective-permute-done((bf16[128,3584]{0,1:T(8,128)(2,1)S(1)}, bf16[128,3584]{0,1:T(8,128)(2,1)}, u32[]{:S(2)}, u32[]{:S(2)}) %collective-permute-start.2) | collective-permute-done | bytes 917536 | tf_op jit(solution)/shard_map/ppermute | solution.py:15
  252.4 1.4 constant_dynamic-update-slice_fusion.7
  253.8 0.3 constant_dynamic-update-slice_fusion.6
  254.1 0.3 constant_dynamic-update-slice_fusion.5
  254.4 0.3 constant_dynamic-update-slice_fusion.4
  254.8 1.5 constant_dynamic-update-slice_fusion.3
  256.3 0.3 constant_dynamic-update-slice_fusion.2
  256.6 0.3 constant_dynamic-update-slice_fusion.1
  256.9 0.3 constant_dynamic-update-slice_fusion
  257.3 2.9 copy-done.3
  260.2 5.4 %fusion = f32[512,1024]{1,0:T(8,128)} fusion(bf16[1024,1792]{1,0:T(8,128)(2,1)S(1)} %copy-done.2, bf16[1024,1792]{1,0:T(8,128)(2,1)S(1)} %copy-done.1, bf16[1024,3584]{0,1:T(8,128)(2,1)S(1)} %constant_dynamic-update-slice_fusion, s32[]{:T(128)S(6)} %select_n.68), kind=kOutput, calls=%fused_computation.8 | convolution fusion | flops 3772776448 | bytes 13107204 | tf_op jit(solution)/shard_map/dot_general | solution.py:40
  265.7 10.0 %convolution_multiply_fusion = f32[1792,1024]{1,0:T(8,128)} fusion(f32[1792,1024]{1,0:T(8,128)} %fusion.13, bf16[512,1792]{0,1:T(8,128)(2,1)} %all-gather.6.cloned.1.call-done, bf16[512,1024]{1,0:T(8,128)(2,1)} %all-gather.8.cloned.1.call-done), kind=kOutput, calls=%fused_computation.9 | convolution fusion | flops 1880883200 | bytes 17563648 | tf_op jit(solution)/shard_map/dot_general | solution.py:34
  275.7 7.5 %convolution_bitcast_fusion = f32[1024,3584]{1,0:T(8,128)} fusion(bf16[512,1024]{1,0:T(8,128)(2,1)S(1)} %copy-done.7, bf16[1024,3584]{0,1:T(8,128)(2,1)S(1)} %copy-done.4, s32[]{:T(128)S(6)} %select_n.68), kind=kOutput, calls=%fused_computation | convolution fusion | flops 3758096384 | bytes 19398660 | tf_op jit(solution)/shard_map/dot_general | solution.py:34
  283.2 14.0 %slice_multiply_fusion = (f32[1024,1792]{1,0:T(8,128)}, f32[1024,1792]{1,0:T(8,128)}) fusion(f32[1024,1792]{1,0:T(8,128)} %get-tuple-element.11, f32[1024,3584]{1,0:T(8,128)} %convolution_bitcast_fusion, f32[1024,1792]{1,0:T(8,128)S(1)} %bitcast.16), kind=kLoop, calls=%fused_computation.1 | loop fusion | flops 3670016 | bytes 44040192 | tf_op jit(solution)/shard_map/mul | solution.py:99
  297.2 20.1 %reduce-scatter.7.cloned.1.call-done = f32[64,1024]{1,0:T(8,128)} async-done(((f32[512,1024]{1,0:T(8,128)}), f32[64,1024]{1,0:T(8,128)}) %reduce-scatter.7.cloned.1.call-update) | async-done | bytes 262160 | tf_op jit(solution)/shard_map/reduce_scatter | solution.py:81
  317.3 1.6 convert_element_type.34
  318.9 69.3 %reduce-scatter.11.cloned.1.call-done = f32[64,1024]{1,0:T(8,128)} async-done(((f32[512,1024]{1,0:T(8,128)}), f32[64,1024]{1,0:T(8,128)}) %reduce-scatter.11.cloned.1.call-update) | async-done | bytes 262160 | tf_op jit(solution)/shard_map/reduce_scatter | solution.py:101
  388.3 1.6 convert_element_type.37
  (27 shorter events, 0.1 us)
Async XLA Ops:
  7.2 46.0 %all-gather.8.cloned.1.call-start = ((), (), s32[]{:S(2)}) async-start(), calls=%async_computation.8 | async-start | bytes 1179648 | tf_op jit(solution)/shard_map/all_gather | solution.py:87
  7.9 86.4 %all-gather.4.cloned.1.call-start = ((), (), s32[]{:S(2)}) async-start(), calls=%async_computation.4 | async-start | bytes 1179648 | tf_op jit(solution)/shard_map/all_gather | solution.py:67
  8.7 128.0 %reduce-scatter.9.cloned.1.call-start = ((), (), s32[]{:S(2)}) async-start(), calls=%async_computation.9 | async-start | bytes 4587520 | tf_op jit(solution)/shard_map/reduce_scatter | solution.py:90
  15.2 46.5 %copy-start.5 = (s32[32,112]{1,0:T(8,128)S(1)}, s32[32,112]{1,0:T(8,128)}, u32[]{:S(2)}) copy-start(s32[32,112]{1,0:T(8,128)} %param.13) | copy-start | bytes 43012
  15.2 47.0 %copy-start.6 = (s32[32,112]{1,0:T(8,128)S(1)}, s32[32,112]{1,0:T(8,128)}, u32[]{:S(2)}) copy-start(s32[32,112]{1,0:T(8,128)} %param.12) | copy-start | bytes 43012
  61.4 142.2 %reduce-scatter.5.cloned.1.call-start = ((), (), s32[]{:S(2)}) async-start(), calls=%async_computation.5 | async-start | bytes 9175040 | tf_op jit(solution)/shard_map/reduce_scatter | solution.py:69
  62.6 7.6 %copy-start = (bf16[1024,1792]{1,0:T(8,128)(2,1)S(1)}, bf16[1024,1792]{1,0:T(8,128)(2,1)}, u32[]{:S(2)}) copy-start(bf16[1024,1792]{1,0:T(8,128)(2,1)} %param.10) | copy-start | bytes 11010052
  105.3 134.2 %all-gather.6.cloned.1.call-start = ((), (), s32[]{:S(2)}) async-start(), calls=%async_computation.6 | async-start | bytes 2293760 | tf_op jit(solution)/shard_map/all_gather | solution.py:79
  206.8 110.5 %reduce-scatter.7.cloned.1.call-start = ((), (), s32[]{:S(2)}) async-start(), calls=%async_computation.7 | async-start | bytes 2359296 | tf_op jit(solution)/shard_map/reduce_scatter | solution.py:81
  206.9 18.9 %collective-permute-start = (bf16[128,3584]{0,1:T(8,128)(2,1)S(1)}, bf16[128,3584]{0,1:T(8,128)(2,1)S(1)}, u32[]{:S(2)}, u32[]{:S(2)}) collective-permute-start(bf16[128,3584]{0,1:T(8,128)(2,1)S(1)} %pad_maximum_fusion.3), channel_id=1, source_target_pairs={{0,1},{1,2},{2,3},{3,0},{4,5},{5,6},{6,7},{7,4},{8,9},{9,10},{10,1... | collective-permute-start | bytes 2752520 | tf_op jit(solution)/shard_map/ppermute | solution.py:15
  225.8 13.6 %collective-permute-start.1 = (bf16[128,3584]{0,1:T(8,128)(2,1)S(1)}, bf16[128,3584]{0,1:T(8,128)(2,1)S(1)}, u32[]{:S(2)}, u32[]{:S(2)}) collective-permute-start(bf16[128,3584]{0,1:T(8,128)(2,1)S(1)} %collective-permute-done), channel_id=1, source_target_pairs={{0,1},{1,2},{2,3},{3,0},{4,5},{5,6},{6,7},{7,4},{8,9},{9,10},{10,1... | collective-permute-start | bytes 2752520 | tf_op jit(solution)/shard_map/ppermute | solution.py:15
  239.4 12.9 %collective-permute-start.2 = (bf16[128,3584]{0,1:T(8,128)(2,1)S(1)}, bf16[128,3584]{0,1:T(8,128)(2,1)}, u32[]{:S(2)}, u32[]{:S(2)}) collective-permute-start(bf16[128,3584]{0,1:T(8,128)(2,1)S(1)} %collective-permute-done.1), channel_id=1, source_target_pairs={{0,1},{1,2},{2,3},{3,0},{4,5},{5,6},{6,7},{7,4},{8,9},{9,10},{10,1... | collective-permute-start | bytes 2752520 | tf_op jit(solution)/shard_map/ppermute | solution.py:15
  247.6 140.6 %reduce-scatter.11.cloned.1.call-start = ((), (), s32[]{:S(2)}) async-start(), calls=%async_computation.10 | async-start | bytes 2359296 | tf_op jit(solution)/shard_map/reduce_scatter | solution.py:101
  247.9 12.3 %copy-start.1 = (bf16[1024,1792]{1,0:T(8,128)(2,1)S(1)}, bf16[1024,1792]{1,0:T(8,128)(2,1)}, u32[]{:S(2)}) copy-start(bf16[1024,1792]{1,0:T(8,128)(2,1)} %get-tuple-element.12) | copy-start | bytes 11010052
  247.9 12.3 %copy-start.2 = (bf16[1024,1792]{1,0:T(8,128)(2,1)S(1)}, bf16[1024,1792]{1,0:T(8,128)(2,1)}, u32[]{:S(2)}) copy-start(bf16[1024,1792]{1,0:T(8,128)(2,1)} %get-tuple-element.10) | copy-start | bytes 11010052
  257.2 2.9 copy-start.3
  265.6 17.6 %slice-start = ((s8[7340032]{0:T(1024)(128)(4,1)}), s8[3145728]{0:T(1024)(128)(4,1)S(1)}, s32[]{:S(2)}) async-start(s8[7340032]{0:T(1024)(128)(4,1)} %bitcast.15), calls=%async_computation.11 | async-start | bytes 6291456
  265.7 10.0 %copy-start.4 = (bf16[1024,3584]{0,1:T(8,128)(2,1)S(1)}, bf16[1024,3584]{0,1:T(8,128)(2,1)}, u32[]{:S(2)}) copy-start(bf16[1024,3584]{0,1:T(8,128)(2,1)} %copy-done.3) | copy-start | bytes 22020100
  265.7 10.0 %copy-start.7 = (bf16[512,1024]{1,0:T(8,128)(2,1)S(1)}, bf16[512,1024]{1,0:T(8,128)(2,1)}, u32[]{:S(2)}) copy-start(bf16[512,1024]{1,0:T(8,128)(2,1)} %all-gather.4.cloned.1.call-done) | copy-start | bytes 3145732
  265.7 17.5 %slice-start.1 = ((s8[7340032]{0:T(1024)(128)(4,1)}), s8[4194304]{0:T(1024)(128)(4,1)S(1)}, s32[]{:S(2)}) async-start(s8[7340032]{0:T(1024)(128)(4,1)} %bitcast.15), calls=%async_computation.12 | async-start | bytes 8388608
Sparse Core Ops, SparseCore 0:
  10.1 42.9 all-gather.7
  55.3 38.9 all-gather.3
  96.8 39.7 reduce-scatter.8
  139.0 64.6 reduce-scatter.4
  206.9 24.7 all-gather.5
  247.7 69.5 reduce-scatter.6
  320.8 67.3 reduce-scatter.10
